TPU v7x, 32 devices: a whole 2x2x4 slice. The times are simulated.
32 devices in a mesh: gx: 4 (over z), gy: 8 (over y, x, core).
Axes of the slice: x: 2, y: 2, z: 4, core: 2. Of those that a mesh axis runs over, the one named last changes fastest.
Arguments:
- populations: float32 [19, 64, 32, 128], P(None, 'gx', 'gy'), as said below
- vert_base: int32 [3, 16384], P(None, ('gx', 'gy')), may hold values from 0 to 127, as said below
- vert_frac: float32 [3, 16384], P(None, ('gx', 'gy')), may hold values from 0 to 0.999
- edges: int32 [2, 49152], P(None, ('gx', 'gy')), may hold values from 0 to 511, as said below
- stiffness: float32 [49152], P(('gx', 'gy')), may hold values from 0.05 to 0.5
- rest: float32 [3, 49152], P(None, ('gx', 'gy')), may hold values from -3 to 3
Outputs:
- fresh: float32 [19, 64, 32, 128], P(None, 'gx', 'gy')
- vertex_velocity: float32 [3, 16384], P(None, ('gx', 'gy'))
Inputs may be any that keep to these rules, and one draw needn't show every extreme that they name: `vert_base`: the first coordinate lies below 64, the second below 32, the third below 128. The vertices are in blocks of 512, block k belonging to the k-th device in the order gx then gy; a vertex's first coordinate lies in that device's 16 cells along x, its second in its 4 cells along y. Each run of 128 vertices of a block lies in a box of 4 x 4 x 4 cells, periodic in z. `edges`: edge e belongs to block e // 1536; its two entries are distinct indices within that block's 512 vertices, both in the same run of 128 vertices. `populations`: every entry lies between 0.6 and 1.4 times the lattice weight of its direction.
All inputs are finite; a program needn't handle non-finite values.
Results may differ from a plain program's by a relative error of at most 0.000078.
Values sent between devices are 32-bit elements; how exact they have to be, the bound alone decides.
A program may use at most 64 MiB of HBM per device.

v0:
```python
import jax
import jax.numpy as jnp
from jax import lax
from jax.experimental import pallas as pl
from jax.experimental.pallas import tpu as pltpu
from jax.sharding import PartitionSpec as P

lattice_speeds = [
    (0, 0, 0),
    (1, 0, 0),
    (-1, 0, 0),
    (0, 1, 0),
    (0, -1, 0),
    (0, 0, 1),
    (0, 0, -1),
    (1, 1, 0),
    (-1, -1, 0),
    (1, -1, 0),
    (-1, 1, 0),
    (1, 0, 1),
    (-1, 0, -1),
    (1, 0, -1),
    (-1, 0, 1),
    (0, 1, 1),
    (0, -1, -1),
    (0, 1, -1),
    (0, -1, 1),
]
lattice_weights = [1.0 / 3.0] + [1.0 / 18.0] * 6 + [1.0 / 36.0] * 12
relax_time = 0.9
run = 128
sides = [(1, 0), (-1, 0), (0, 1), (0, -1), (1, 1), (1, -1), (-1, 1), (-1, -1)]
f32, bf16 = jnp.float32, jnp.bfloat16


def outer_weight(r):
    return (5.0 - 2.0 * r - jnp.sqrt(-7.0 + 12.0 * r - 4.0 * r * r)) / 8.0


def inner_weight(r):
    return (3.0 - 2.0 * r + jnp.sqrt(1.0 + 4.0 * r - 4.0 * r * r)) / 8.0


def up8(n):
    return (n + 7) // 8 * 8


class Plan:
    def __init__(self, wx, wy):
        self.wx, self.wy = wx, wy
        self.own = wx * wy
        self.xh = self.own
        self.yh = self.xh + 4 * wy
        self.co = self.yh + 3 * wx
        self.rows = self.co + 16
        hx, hy = [-1, wx, wx + 1], [-1, wy, wy + 1]
        self.row = {}
        for x in range(wx):
            for y in range(wy):
                self.row[x, y] = x * wy + y
        for k in range(3):
            for y in range(wy):
                self.row[hx[k], y] = self.xh + k * wy + y
            for x in range(wx):
                self.row[x, hy[k]] = self.yh + k * wx + x
            for m in range(3):
                self.row[hx[m], hy[k]] = self.co + 3 * k + m
        self.pads = [(self.xh + 3 * wy, wy), (self.co + 9, 7)]

        def span(d, w):
            full = list(range(w)) + [-1, w, w + 1]
            return {0: full, 1: [w - 1, w, w + 1], -1: [-1, 0, 1]}[d]

        def edge(d, w):
            return {0: list(range(w)), 1: [w - 1], -1: [0, 1]}[d]

        def near(d, w):
            return {0: list(range(w)), 1: [w - 1], -1: [0]}[d]

        def cells(d, pick):
            xs, ys = pick(d[0], wx), pick(d[1], wy)
            if d[1]:
                return [(x, y) for y in ys for x in xs]
            return [(x, y) for x in xs for y in ys]

        self.force = [cells(d, span) for d in sides]
        self.edge = [cells(d, edge) for d in sides]
        self.near = [cells(d, near) for d in sides]
        self.dirs = [
            [
                q
                for q, c in enumerate(lattice_speeds)
                if (not d[0] or c[0] == d[0]) and (not d[1] or c[1] == d[1])
            ]
            for d in sides
        ]
        self.force_rows = [up8(3 * len(c)) for c in self.force]
        self.macro_rows = [
            up8(4 * len(e) + len(q) * len(n)) for e, q, n in zip(self.edge, self.dirs, self.near)
        ]

    def there(self, cell, d):
        return self.row[cell[0] - d[0] * self.wx, cell[1] - d[1] * self.wy]


def runs(src, dst):
    out, i = [], 0
    while i < len(src):
        n, a, b = 1, 1, 1
        if i + 1 < len(src) and src[i + 1] > src[i] and dst[i + 1] > dst[i]:
            a, b = src[i + 1] - src[i], dst[i + 1] - dst[i]
            n = 2
            while i + n < len(src) and src[i + n] - src[i + n - 1] == a and dst[i + n] - dst[i + n - 1] == b:
                n += 1
        out.append((src[i], a, dst[i], b, n))
        i += n
    return out


def ds(start, n, stride):
    return pl.ds(start, n, stride=stride) if stride > 1 else pl.ds(start, n)


def move(src_ref, src, dst_ref, dst, add=False):
    for s, a, d, b, n in runs(src, dst):
        value = src_ref[ds(s, n, a), :]
        if add:
            value = value + dst_ref[ds(d, n, b), :]
        dst_ref[ds(d, n, b), :] = value


def split(value):
    high = value.astype(bf16)
    return high, (value - high.astype(f32)).astype(bf16)


def pick4(delta, weights):
    out = jnp.zeros(delta.shape, f32)
    for k in range(4):
        out = jnp.where(delta == k, weights[k], out)
    return out


def exchange_kernel(plan, nx, ny, *refs):
    wx, wy, rows, own = plan.wx, plan.wy, plan.rows, plan.own
    sources, results, scratch = refs[0:6], refs[6:12], refs[12:]
    pops, ext, grid, halo, plane, along = results
    ms, mr, fs, fr = scratch[0:8], scratch[8:16], scratch[16:24], scratch[24:32]
    base, frac, edges, stiff, rest, pos, pull, mem, sems, load_sems = scratch[32:]
    targets = (pops, base, frac, edges, stiff, rest)
    loads_in = [pltpu.make_async_copy(sources[n], targets[n], load_sems.at[n]) for n in range(6)]
    for n in (3, 2, 1, 5, 4, 0):
        loads_in[n].start()
    count, depth = base.shape[1], pops.shape[1]
    edge_count = edges.shape[1]
    tiles = count // run
    ix, iy = lax.axis_index("gx"), lax.axis_index("gy")
    peers = [(lax.rem(ix + dx + nx, nx), lax.rem(iy + dy + ny, ny)) for dx, dy in sides]
    barrier = pltpu.get_barrier_semaphore()
    for peer in peers:
        pl.semaphore_signal(barrier, inc=1, device_id=peer, device_id_type=pl.DeviceIdType.MESH)

    def copies(src, dst, kind):
        return [
            pltpu.make_async_remote_copy(
                src_ref=src[n],
                dst_ref=dst[n],
                send_sem=sems.at[kind, n],
                recv_sem=sems.at[kind + 1, n],
                device_id=peers[n],
                device_id_type=pl.DeviceIdType.MESH,
            )
            for n in range(8)
        ]

    macro_copies = copies(ms, mr, 0)
    force_copies = copies(fs, fr, 2)

    pos[...] = jnp.zeros(pos.shape, f32)
    pull[...] = jnp.zeros(pull.shape, f32)
    for n in (3, 2, 1, 5, 4):
        loads_in[n].wait()
    part = 8 * tiles
    moved = frac[...]
    high = moved.astype(bf16).astype(f32)
    low = moved - high
    whole = base[...].astype(f32)
    for t in range(tiles):
        cols = slice(t * run, (t + 1) * run)
        pos[pl.ds(8 * t, 3), :] = whole[:, cols]
        pos[pl.ds(part + 8 * t, 3), :] = high[:, cols]
        pos[pl.ds(2 * part + 8 * t, 3), :] = low[:, cols]
    ends = edges[...]
    spot = lax.broadcasted_iota(jnp.int32, (run, edge_count), 0)
    tail = jnp.bitwise_and(ends[0:1], run - 1)
    head = jnp.bitwise_and(ends[1:2], run - 1)
    hot = (jnp.where(spot == head, 1.0, 0.0) - jnp.where(spot == tail, 1.0, 0.0)).astype(bf16)
    group = lax.shift_right_logical(ends[0:1], run.bit_length() - 1)
    reach = jnp.dot(pos[...].astype(bf16), hot, preferred_element_type=f32)
    reach = reach[0:part] + reach[part : 2 * part] + reach[2 * part : 3 * part]
    pull[pl.ds(0, 3), :] = rest[...]
    diff = jnp.zeros((8, edge_count), f32)
    for t in range(tiles):
        diff = jnp.where(group == t, reach[8 * t : 8 * t + 8], diff)
    stretch = stiff[...].reshape(1, edge_count) * (diff - pull[...])
    terms = jnp.concatenate([jnp.where(group == t, stretch, 0.0) for t in range(tiles)], axis=0)
    big, small = split(terms)
    both = jnp.concatenate([big, small], axis=0)
    summed = lax.dot_general(both, hot, (((1,), (1,)), ((), ())), preferred_element_type=f32)
    summed = summed[0:part] + summed[part : 2 * part]
    for t in range(tiles):
        mem[:, t * run : (t + 1) * run] = -summed[8 * t : 8 * t + 8]

    loads_in[0].wait()
    for r in range(0, own, 16):
        totals = [None] * 4
        for q, c in enumerate(lattice_speeds):
            value = pops[pl.ds(q * own + r, 16), :]
            for k, sign in enumerate((1,) + c):
                if sign:
                    term = value if sign > 0 else -value
                    totals[k] = term if totals[k] is None else totals[k] + term
        for k in range(4):
            ext[pl.ds(k * rows + r, 16), :] = totals[k]
    for start, n in plan.pads:
        for k in range(4):
            ext[pl.ds(k * rows + start, n), :] = jnp.full((n, depth), 0.0 if k else 1.0, f32)
    for n in range(8):
        cells, close = plan.edge[n], plan.near[n]
        for k in range(4):
            move(ext, [k * rows + plan.row[c] for c in cells], ms[n], [k * len(cells) + i for i in range(len(cells))])
        for s, q in enumerate(plan.dirs[n]):
            first = 4 * len(cells) + s * len(close)
            move(pops, [q * own + plan.row[c] for c in close], ms[n], [first + i for i in range(len(close))])

    pl.semaphore_wait(barrier, 8)
    for copy in macro_copies:
        copy.start()

    weights = [
        outer_weight(1.0 + moved),
        inner_weight(moved),
        inner_weight(1.0 - moved),
        outer_weight(2.0 - moved),
    ]
    bx = base[0:1, :] - ix * wx - 1
    by = base[1:2, :] - iy * wy - 1
    bz = base[2:3, :] - 1
    gap = lax.broadcasted_iota(jnp.int32, (depth, count), 0) - bz
    gap = jnp.where(gap < 0, gap + depth, gap)
    gap = jnp.where(gap >= depth, gap - depth, gap)
    along_z = pick4(gap, [w[2:3] for w in weights])
    z_high, z_low = split(along_z)
    along[pl.ds(0, depth), :] = z_high
    along[pl.ds(depth, depth), :] = z_low
    far = -100
    for r in range(0, rows, 16):
        i = lax.broadcasted_iota(jnp.int32, (16, 1), 0)
        if r < plan.xh:
            i = i + r
            x = i // wy
            y = i - x * wy
        elif r < plan.yh:
            i = i + (r - plan.xh)
            k = i // wy
            x = jnp.where(k == 0, -1, jnp.where(k == 3, far, wx - 1 + k))
            y = i - k * wy
        elif r < plan.co:
            k = (r - plan.yh) // wx
            x = i + (r - plan.yh - k * wx)
            y = jnp.full((16, 1), (-1, wy, wy + 1)[k], jnp.int32)
        else:
            k = jnp.where(i >= 6, 2, jnp.where(i >= 3, 1, 0))
            m = i - 3 * k
            x = jnp.where(m == 0, -1, jnp.where(m >= 3, far, wx - 1 + m))
            y = jnp.where(k == 0, -1, wy - 1 + k)
        px = pick4(x - bx, [w[0:1] for w in weights])
        py = pick4(y - by, [w[1:2] for w in weights])
        plane[pl.ds(r, 16), :] = px * py
    flat = plane[...]
    loads = [split(flat * mem[c : c + 1, :]) for c in range(3)]
    stack = jnp.concatenate([h for h, _ in loads] + [l for _, l in loads], axis=0)
    spread = lax.dot_general(stack, along[...], (((1,), (1,)), ((), ())), preferred_element_type=f32)
    spread = spread[0 : 3 * rows] + spread[3 * rows : 6 * rows]
    grid[...] = spread[:, 0:depth] + spread[:, depth : 2 * depth]
    for n in range(8):
        cells = plan.force[n]
        for k in range(3):
            move(grid, [k * rows + plan.row[c] for c in cells], fs[n], [k * len(cells) + i for i in range(len(cells))])
    for copy in force_copies:
        copy.start()

    for n in range(8):
        macro_copies[n].wait_recv()
        cells, close, d = plan.edge[n], plan.near[n], sides[n]
        for k in range(4):
            move(mr[n], [k * len(cells) + i for i in range(len(cells))], ext, [k * rows + plan.there(c, d) for c in cells])
        for s, q in enumerate(plan.dirs[n]):
            first = 4 * len(cells) + s * len(close)
            move(mr[n], [first + i for i in range(len(close))], halo, [q * rows + plan.there(c, d) for c in close])
    for n in range(8):
        force_copies[n].wait_recv()
        cells, d = plan.force[n], sides[n]
        for k in range(3):
            move(fr[n], [k * len(cells) + i for i in range(len(cells))], grid, [k * rows + plan.there(c, d) for c in cells], add=True)

    for copy in macro_copies + force_copies:
        copy.wait_send()


def collide_kernel(plan, pops, ext, grid, halo, plane, along, fresh_out, sampled_out, *scratch):
    wx, wy, rows, own = plan.wx, plan.wy, plan.rows, plan.own
    fresh, sampled, post, vel, sems = scratch
    depth = pops.shape[1]
    leave = [
        pltpu.make_async_copy(
            fresh.at[pl.ds(q * own, own), :], fresh_out.at[pl.ds(q * own, own), :], sems.at[q]
        )
        for q in range(19)
    ]
    leave.append(pltpu.make_async_copy(sampled, sampled_out, sems.at[19]))
    keep = 1.0 - 1.0 / relax_time
    half = 1.0 - 0.5 / relax_time

    def along_speed(c, vector):
        total = None
        for k in range(3):
            if c[k]:
                term = vector[k] if c[k] > 0 else -vector[k]
                total = term if total is None else total + term
        return total

    for r in range(0, rows, 16):
        density = ext[pl.ds(r, 16), :]
        force = [grid[pl.ds(k * rows + r, 16), :] for k in range(3)]
        inverse = 1.0 / density
        speed = [(ext[pl.ds((k + 1) * rows + r, 16), :] + 0.5 * force[k]) * inverse for k in range(3)]
        for k in range(3):
            vel[pl.ds(k * rows + r, 16), :] = speed[k]
        if r < own:
            need = list(range(19))
        elif r < plan.yh:
            need = [q for q in range(19) if lattice_speeds[q][0]]
        elif r < plan.yh + wx:
            need = [q for q in range(19) if lattice_speeds[q][1] == 1]
        elif r < plan.yh + 2 * wx:
            need = [q for q in range(19) if lattice_speeds[q][1] == -1]
        elif r < plan.co:
            continue
        else:
            need = [q for q in range(19) if lattice_speeds[q][0] and lattice_speeds[q][1]]
        square = speed[0] * speed[0] + speed[1] * speed[1] + speed[2] * speed[2]
        work = speed[0] * force[0] + speed[1] * force[1] + speed[2] * force[2]
        scaled = density * (1.0 / relax_time)
        level = scaled * (1.0 - 1.5 * square) - (3.0 * half) * work
        for first in [0] + list(range(1, 19, 2)):
            pair = [0] if first == 0 else [first, first + 1]
            if not any(q in need for q in pair):
                continue
            weight = lattice_weights[first]
            if first == 0:
                even, odd = level * weight, None
            else:
                a = along_speed(lattice_speeds[first], speed)
                push = along_speed(lattice_speeds[first], force)
                turn = scaled * a + half * push
                even = weight * (level + a * (4.5 * scaled * a + 9.0 * half * push))
                odd = (3.0 * weight) * turn
            for q in pair:
                if q not in need:
                    continue
                c = lattice_speeds[q]
                if r < own:
                    value = pops[pl.ds(q * own + r, 16), :]
                else:
                    value = halo[pl.ds(q * rows + r, 16), :]
                value = keep * value + even
                if odd is not None:
                    value = value + odd if q == first else value - odd
                if c[2]:
                    value = pltpu.roll(value, c[2] % depth, 1)
                if c[0] == 0 and c[1] == 0:
                    fresh[pl.ds(q * own + r, 16), :] = value
                else:
                    post[pl.ds(q * rows + r, 16), :] = value
    for q, c in enumerate(lattice_speeds):
        if c[0] == 0 and c[1] == 0:
            leave[q].start()
            continue
        if c[1]:
            cells = [(x, y) for y in range(wy) for x in range(wx)]
        else:
            cells = [(x, y) for x in range(wx) for y in range(wy)]
        move(
            post,
            [q * rows + plan.row[x - c[0], y - c[1]] for x, y in cells],
            fresh,
            [q * own + x * wy + y for x, y in cells],
        )
        leave[q].start()

    v_high, v_low = split(vel[...])
    value = jnp.dot(v_high, along[pl.ds(0, depth), :], preferred_element_type=f32)
    value = value + jnp.dot(v_low, along[pl.ds(0, depth), :], preferred_element_type=f32)
    value = value + jnp.dot(v_high, along[pl.ds(depth, depth), :], preferred_element_type=f32)
    flat = plane[...]
    for k in range(3):
        sampled[k : k + 1, :] = jnp.sum(value[k * rows : (k + 1) * rows] * flat, axis=0, keepdims=True)
    leave[19].start()
    for copy in leave:
        copy.wait()


def solution(mesh):
    nx, ny = mesh.shape["gx"], mesh.shape["gy"]

    def per_device(populations, vert_base, vert_frac, edges, stiffness, rest):
        _, wx, wy, depth = populations.shape
        count, edge_count = vert_base.shape[1], edges.shape[1]
        plan = Plan(wx, wy)
        rows, tiles = plan.rows, count // run
        macro = [pltpu.VMEM((n, depth), f32) for n in plan.macro_rows]
        force = [pltpu.VMEM((n, depth), f32) for n in plan.force_rows]
        scratch = macro + macro + force + force
        scratch += [
            pltpu.VMEM((3, count), jnp.int32),
            pltpu.VMEM((3, count), f32),
            pltpu.VMEM((2, edge_count), jnp.int32),
            pltpu.VMEM((edge_count,), f32),
            pltpu.VMEM((3, edge_count), f32),
            pltpu.VMEM((24 * tiles, run), f32),
            pltpu.VMEM((8, edge_count), f32),
            pltpu.VMEM((8, count), f32),
            pltpu.SemaphoreType.DMA((4, 8)),
            pltpu.SemaphoreType.DMA((6,)),
        ]
        vmem = pl.BlockSpec(memory_space=pltpu.VMEM)
        far = pl.BlockSpec(memory_space=pltpu.HBM)

        def exchange(*refs):
            exchange_kernel(plan, nx, ny, *refs)

        def collide(*refs):
            collide_kernel(plan, *refs)

        held = pl.pallas_call(
            exchange,
            out_shape=(
                jax.ShapeDtypeStruct((19 * wx * wy, depth), f32),
                jax.ShapeDtypeStruct((4 * rows, depth), f32),
                jax.ShapeDtypeStruct((3 * rows, depth), f32),
                jax.ShapeDtypeStruct((19 * rows, depth), f32),
                jax.ShapeDtypeStruct((rows, count), f32),
                jax.ShapeDtypeStruct((2 * depth, count), bf16),
            ),
            in_specs=[far] * 6,
            out_specs=(vmem,) * 6,
            scratch_shapes=scratch,
            compiler_params=pltpu.CompilerParams(
                collective_id=0, has_side_effects=True, vmem_limit_bytes=24 * 1024 * 1024
            ),
            name="exchange",
        )(
            *[
                pltpu.with_memory_space_constraint(value, pltpu.HBM)
                for value in (
                    populations.reshape(19 * wx * wy, depth),
                    vert_base,
                    vert_frac,
                    edges,
                    stiffness,
                    rest,
                )
            ]
        )
        fresh, sampled = pl.pallas_call(
            collide,
            out_shape=(
                jax.ShapeDtypeStruct((19 * wx * wy, depth), f32),
                jax.ShapeDtypeStruct((3, count), f32),
            ),
            in_specs=[vmem] * 6,
            out_specs=(far, far),
            scratch_shapes=[
                pltpu.VMEM((19 * wx * wy, depth), f32),
                pltpu.VMEM((3, count), f32),
                pltpu.VMEM((19 * rows, depth), f32),
                pltpu.VMEM((3 * rows, depth), f32),
                pltpu.SemaphoreType.DMA((20,)),
            ],
            compiler_params=pltpu.CompilerParams(vmem_limit_bytes=24 * 1024 * 1024),
            name="collide",
        )(*held)
        return fresh.reshape(19, wx, wy, depth), sampled

    placed = (
        P(None, "gx", "gy", None),
        P(None, ("gx", "gy")),
        P(None, ("gx", "gy")),
        P(None, ("gx", "gy")),
        P(("gx", "gy")),
        P(None, ("gx", "gy")),
    )
    return jax.shard_map(
        per_device,
        mesh=mesh,
        in_specs=placed,
        out_specs=(P(None, "gx", "gy", None), P(None, ("gx", "gy"))),
        check_vma=False,
    )
```

profile of v0, /device:TPU:0, one launch (start us, length us, event | category | flops | bytes accessed | tf_op | source)
XLA Modules:
  0.0 15.0 jit_solution(9017601025784775586)
XLA Ops:
  0.6 12.9 %exchange.1 = (f32[1216,128]{1,0:T(8,128)S(1)}, f32[576,128]{1,0:T(8,128)S(1)}, f32[432,128]{1,0:T(8,128)S(1)}, f32[2736,128]{1,0:T(8,128)S(1)}, f32[144,512]{1,0:T(8,128)S(1)}, /*index=5*/bf16[256,512]{1,0:T(8,128)(2,1)S(1)}) custom-call(f32[1216,128]{1,0:T(8,128)} %bitcast.2, s32[3,512]{1,0:T(4,128)} %refs_1_.1, f32[3,512]{1,0:T(4,128)} %refs_2_.1, ...), custom_call_target="tpu_custom_call" | custom-call | tf_op jit(solution)/shard_map/exchange/pallas_call | solution.py:446
  13.5 1.4 %collide.1 = (f32[1216,128]{1,0:T(8,128)}, f32[3,512]{1,0:T(4,128)}) custom-call(f32[1216,128]{1,0:T(8,128)S(1)} %get-tuple-element.10.refs_0_, f32[576,128]{1,0:T(8,128)S(1)} %get-tuple-element.11.refs_1_, f32[432,128]{1,0:T(8,128)S(1)} %get-tuple-element.12.refs_2_, f32[2736,128]{1,0:T(8,128)S(1)} %get-tuple-element.13.refs_3_, ...), custom_call_target="tpu_custom_call" | custom-call | tf_op jit(solution)/shard_map/collide/pallas_call | solution.py:476
where the time goes:
time: 15.2 us; the launch traced here: 15 us
  Pallas kernels  14.3 us (94%)
  between operations  0.64 us (4%)
    pallas_call x1, Pallas kernels, per_device(): pl.pallas_call(exchange, out_shape=(jax.ShapeDtypeStruct((19 * wx * wy, d...  12.9 us
    pallas_call x1, Pallas kernels, per_device(): pl.pallas_call(collide, out_shape=(jax.ShapeDtypeStruct((19 * wx * wy, de...  1.43 us

commit v1 on v0

--- a/solution.py
+++ b/solution.py
@@ -29,7 +29,7 @@
 lattice_weights = [1.0 / 3.0] + [1.0 / 18.0] * 6 + [1.0 / 36.0] * 12
 relax_time = 0.9
 run = 128
-sides = [(1, 0), (-1, 0), (0, 1), (0, -1), (1, 1), (1, -1), (-1, 1), (-1, -1)]
+sides = [(1, 1), (1, -1), (-1, 1), (-1, -1), (0, 1), (0, -1), (1, 0), (-1, 0)]
 f32, bf16 = jnp.float32, jnp.bfloat16
 
 
@@ -210,32 +210,6 @@
     summed = summed[0:part] + summed[part : 2 * part]
     for t in range(tiles):
         mem[:, t * run : (t + 1) * run] = -summed[8 * t : 8 * t + 8]
-
-    loads_in[0].wait()
-    for r in range(0, own, 16):
-        totals = [None] * 4
-        for q, c in enumerate(lattice_speeds):
-            value = pops[pl.ds(q * own + r, 16), :]
-            for k, sign in enumerate((1,) + c):
-                if sign:
-                    term = value if sign > 0 else -value
-                    totals[k] = term if totals[k] is None else totals[k] + term
-        for k in range(4):
-            ext[pl.ds(k * rows + r, 16), :] = totals[k]
-    for start, n in plan.pads:
-        for k in range(4):
-            ext[pl.ds(k * rows + start, n), :] = jnp.full((n, depth), 0.0 if k else 1.0, f32)
-    for n in range(8):
-        cells, close = plan.edge[n], plan.near[n]
-        for k in range(4):
-            move(ext, [k * rows + plan.row[c] for c in cells], ms[n], [k * len(cells) + i for i in range(len(cells))])
-        for s, q in enumerate(plan.dirs[n]):
-            first = 4 * len(cells) + s * len(close)
-            move(pops, [q * own + plan.row[c] for c in close], ms[n], [first + i for i in range(len(close))])
-
-    pl.semaphore_wait(barrier, 8)
-    for copy in macro_copies:
-        copy.start()
 
     weights = [
         outer_weight(1.0 + moved),
@@ -287,6 +261,32 @@
         cells = plan.force[n]
         for k in range(3):
             move(grid, [k * rows + plan.row[c] for c in cells], fs[n], [k * len(cells) + i for i in range(len(cells))])
+    loads_in[0].wait()
+    for r in range(0, own, 16):
+        totals = [None] * 4
+        for q, c in enumerate(lattice_speeds):
+            value = pops[pl.ds(q * own + r, 16), :]
+            for k, sign in enumerate((1,) + c):
+                if sign:
+                    term = value if sign > 0 else -value
+                    totals[k] = term if totals[k] is None else totals[k] + term
+        for k in range(4):
+            ext[pl.ds(k * rows + r, 16), :] = totals[k]
+    for start, n in plan.pads:
+        for k in range(4):
+            ext[pl.ds(k * rows + start, n), :] = jnp.full((n, depth), 0.0 if k else 1.0, f32)
+    for n in range(8):
+        cells, close = plan.edge[n], plan.near[n]
+        for k in range(4):
+            move(ext, [k * rows + plan.row[c] for c in cells], ms[n], [k * len(cells) + i for i in range(len(cells))])
+        for s, q in enumerate(plan.dirs[n]):
+            first = 4 * len(cells) + s * len(close)
+            move(pops, [q * own + plan.row[c] for c in close], ms[n], [first + i for i in range(len(close))])
+
+    pl.semaphore_wait(barrier, 8)
+    for copy in macro_copies:
+        copy.start()
+
     for copy in force_copies:
         copy.start()
 

time: 15.2 us -> 14.9 us (0.980)
  Pallas kernels: 14.3 us -> 14 us
    pallas_call x1, Pallas kernels: 12.9 us -> 12.6 us  [per_device(): pl.pallas_call(exchange, out_shape=(jax.ShapeDtypeStruct((19 * wx * wy, d...]
where the time goes in v1:
time: 14.9 us; the launch traced here: 14.7 us
  Pallas kernels  14 us (94%)
  between operations  0.64 us (4%)
    pallas_call x1, Pallas kernels, per_device(): pl.pallas_call(exchange, out_shape=(jax.ShapeDtypeStruct((19 * wx * wy, d...  12.6 us
    pallas_call x1, Pallas kernels, per_device(): pl.pallas_call(collide, out_shape=(jax.ShapeDtypeStruct((19 * wx * wy, de...  1.43 us

profile of v1, /device:TPU:0, one launch (start us, length us, event | category | flops | bytes accessed | tf_op | source)
XLA Modules:
  0.0 14.7 jit_solution(2360430269210437932)
XLA Ops:
  0.6 12.6 %exchange.1 = (f32[1216,128]{1,0:T(8,128)S(1)}, f32[576,128]{1,0:T(8,128)S(1)}, f32[432,128]{1,0:T(8,128)S(1)}, f32[2736,128]{1,0:T(8,128)S(1)}, f32[144,512]{1,0:T(8,128)S(1)}, /*index=5*/bf16[256,512]{1,0:T(8,128)(2,1)S(1)}) custom-call(f32[1216,128]{1,0:T(8,128)} %bitcast.2, s32[3,512]{1,0:T(4,128)} %refs_1_.1, f32[3,512]{1,0:T(4,128)} %refs_2_.1, ...), custom_call_target="tpu_custom_call" | custom-call | tf_op jit(solution)/shard_map/exchange/pallas_call | solution.py:446
  13.2 1.4 %collide.1 = (f32[1216,128]{1,0:T(8,128)}, f32[3,512]{1,0:T(4,128)}) custom-call(f32[1216,128]{1,0:T(8,128)S(1)} %get-tuple-element.10.refs_0_, f32[576,128]{1,0:T(8,128)S(1)} %get-tuple-element.11.refs_1_, f32[432,128]{1,0:T(8,128)S(1)} %get-tuple-element.12.refs_2_, f32[2736,128]{1,0:T(8,128)S(1)} %get-tuple-element.13.refs_3_, ...), custom_call_target="tpu_custom_call" | custom-call | tf_op jit(solution)/shard_map/collide/pallas_call | solution.py:476
